TPU v7x, 32 devices: a whole 2x2x4 slice. The times are simulated.
32 devices in a mesh: dp: 8 (over y, x, core), tensor: 4 (over z).
Axes of the slice: x: 2, y: 2, z: 4, core: 2. Of those that a mesh axis runs over, the one named last changes fastest.
Arguments:
- block_input: float32 [12544, 512], P(('dp', 'tensor')), as said below
- cotangent: float32 [12544, 512], P(('dp', 'tensor')), may hold values from -6 to 6
- w_qkv: bfloat16 [2, 512, 3, 512], P(None, 'dp', None, 'tensor'), may hold values from -0.25 to 0.25
- b_qv: bfloat16 [2, 2, 512], P(None, None, 'tensor'), may hold values from -3 to 3
- bias_table: bfloat16 [2, 169, 16], P(None, None, 'tensor'), may hold values from -4 to 4
- w_proj: bfloat16 [2, 512, 512], P(None, 'tensor', 'dp'), may hold values from -0.75 to 0.75
- w_fc1: bfloat16 [2, 512, 2048], P(None, 'dp', 'tensor'), may hold values from -0.25 to 0.25
- b_fc1: bfloat16 [2, 2048], P(None, 'tensor'), may hold values from -3 to 3
- w_fc2: bfloat16 [2, 2048, 512], P(None, 'tensor', 'dp'), may hold values from -0.1875 to 0.1875
- norm_params: bfloat16 [2, 6, 512], P(None, None, 'dp'), as said below
- rel_index: int32 [49, 49], replicated, may hold values from 0 to 168, as said below
- shift_perm: int32 [196], replicated, may hold values from 0 to 195, as said below
- shift_mask: int32 [4, 49, 49], replicated, may hold values from 0 to 1, as said below
Outputs:
- block_output: float32 [12544, 512], P(('dp', 'tensor'))
- d_block_input: float32 [12544, 512], P(('dp', 'tensor'))
- d_w_qkv: float32 [2, 512, 3, 512], P(None, 'dp', None, 'tensor')
- d_b_qv: float32 [2, 2, 512], P(None, None, 'tensor')
- d_bias_table: float32 [2, 169, 16], P(None, None, 'tensor')
- d_w_proj: float32 [2, 512, 512], P(None, 'tensor', 'dp')
- d_w_fc1: float32 [2, 512, 2048], P(None, 'dp', 'tensor')
- d_b_fc1: float32 [2, 2048], P(None, 'tensor')
- d_w_fc2: float32 [2, 2048, 512], P(None, 'tensor', 'dp')
- d_norm_params: float32 [2, 6, 512], P(None, None, 'dp')
Inputs may be any that keep to these rules, and one draw needn't show every extreme that they name: `block_input`: standard normal scaled by a factor per token and a factor per feature. `norm_params`: rows 0 and 3 are positive gains. `rel_index`: two pairs of window positions have equal entries exactly when they have the same row offset and the same column offset; every value appears. A permutation: the image is rolled cyclically by amounts of 1 to 6 tokens, drawn once, along both grid dimensions, and cut into windows; window-ordered position j of the rolled image holds the token whose window-ordered position is shift_perm[j]. `shift_mask`: 1 where two positions of a window of the rolled image of shift_perm lie in different regions of the shifted-window partition for that roll, else 0; zero on the diagonal.
All inputs are finite; a program needn't handle non-finite values.
Results may differ from a plain program's by a relative error of at most 0.022.
Values may be sent and summed in bfloat16 or wider, within the bound.
No kernel may reach another device: no remote copies, remote signals or barrier semaphores. Data moves between devices by JAX's collectives and lax.ppermute only.
A program may use at most 192 MiB of HBM per device.

v0:
```python
import jax
import jax.numpy as jnp
from jax import lax
from jax.sharding import PartitionSpec as P

D = 512
HEAD_DIM = 32
WTOK = 49
ITOK = 196
NWIN = 4
RELS = 169


EPS = 1e-05
MASKED = -100.0
ROOT_HALF = 0.7071067811865476
ROOT_TWO_PI = 2.5066282746310002
full_precision = lax.Precision.HIGHEST


def gelu_value(inputs):
    return inputs * 0.5 * (1.0 + lax.erf(inputs * ROOT_HALF))


def gelu_slope(inputs):
    return (
        0.5 * (1.0 + lax.erf(inputs * ROOT_HALF))
        + inputs * jnp.exp(-0.5 * inputs * inputs) / ROOT_TWO_PI
    )


def layer_norm(hidden, norm_gain, offset):
    row_mean = jnp.mean(hidden, axis=-1, keepdims=True)
    centred = hidden - row_mean
    inv_std = lax.rsqrt(jnp.mean(centred * centred, axis=-1, keepdims=True) + EPS)
    normed = centred * inv_std
    return (normed * norm_gain + offset, normed, inv_std)


def norm_back(grad_rows, normed, inv_std, norm_gain):
    scaled = grad_rows * norm_gain
    centred_grad = (
        scaled
        - jnp.mean(scaled, axis=-1, keepdims=True)
        - normed * jnp.mean(scaled * normed, axis=-1, keepdims=True)
    )
    return inv_std * centred_grad


def inner_rows(left_side, right_side):
    return lax.dot_general(
        left_side, right_side, (((0,), (0,)), ((), ())), preferred_element_type=jnp.float32
    )


def times_transposed(left_side, right_side):
    return lax.dot_general(
        left_side, right_side, (((1,), (1,)), ((), ())), preferred_element_type=jnp.float32
    )


def rel_lookup(rel_index):
    flat_cells = rel_index.reshape(-1)
    return (flat_cells[:, None] == jnp.arange(RELS, dtype=jnp.int32)[None, :]).astype(jnp.float32)


def position_bias(lookup, pos_table):
    head_count = pos_table.shape[-1]
    flat_bias = jnp.dot(lookup, pos_table.astype(jnp.float32), precision=full_precision)
    return flat_bias.reshape(WTOK, WTOK, head_count).transpose(2, 0, 1)


def window_scores(query_blocks, key_blocks, pos_bias, mask_term):
    scores = jnp.einsum(
        "inqhe,inkhe->inhqk", query_blocks, key_blocks, preferred_element_type=jnp.float32
    )
    scores = scores + pos_bias[None, None]
    if mask_term is not None:
        scores = scores + mask_term[None, :, None]
    return scores


def spread_rows(values):
    return lax.all_gather(values, "tensor", axis=0, tiled=True)


def spread_grads(values):
    return lax.all_gather(values, "tensor", axis=0, tiled=True)


def branch_sum(values, weight):
    return lax.psum_scatter(
        jnp.dot(values, weight, preferred_element_type=jnp.float32).astype(jnp.bfloat16),
        "tensor",
        scatter_dimension=0,
        tiled=True,
    ).astype(jnp.float32)


def back_sum(values, weight):
    return lax.psum_scatter(
        times_transposed(values, weight).astype(jnp.bfloat16),
        "tensor",
        scatter_dimension=0,
        tiled=True,
    ).astype(jnp.float32)


def forward_layer(hidden, weights, lookup, mask_term, reorder):
    w_qkv, b_qv, pos_table, w_proj, w_fc1, b_fc1, w_fc2, norm_rows = weights
    norm_rows = norm_rows.astype(jnp.float32)
    local_width = w_qkv.shape[-1]
    head_count = local_width // HEAD_DIM
    score_scale = HEAD_DIM ** (-0.5)
    ln_first, normed_first, inv_first = layer_norm(hidden, norm_rows[0], norm_rows[1])
    gathered = spread_rows(ln_first.astype(jnp.bfloat16))
    image_count = gathered.shape[0] // ITOK
    arranged = gathered.reshape(image_count, ITOK, D)
    if reorder is not None:
        arranged = jnp.take(arranged, reorder[0], axis=1)
    permuted_rows = arranged.reshape(image_count * ITOK, D)
    projected = jnp.dot(
        permuted_rows, w_qkv.reshape(D, 3 * local_width), preferred_element_type=jnp.float32
    )
    projected = projected.reshape(-1, 3, local_width)
    biases = b_qv.astype(jnp.float32)
    query_rows = ((projected[:, 0] + biases[0]) * score_scale).astype(jnp.bfloat16)
    key_rows = projected[:, 1].astype(jnp.bfloat16)
    value_rows = (projected[:, 2] + biases[1]).astype(jnp.bfloat16)
    block_shape = (image_count, NWIN, WTOK, head_count, HEAD_DIM)
    query_blocks = query_rows.reshape(block_shape)
    key_blocks = key_rows.reshape(block_shape)
    value_blocks = value_rows.reshape(block_shape)
    pos_bias = position_bias(lookup, pos_table)
    scores = window_scores(query_blocks, key_blocks, pos_bias, mask_term)
    row_peak = jnp.max(scores, axis=-1, keepdims=True)
    log_total = row_peak + jnp.log(jnp.sum(jnp.exp(scores - row_peak), axis=-1, keepdims=True))
    soft_weights = jnp.exp(scores - log_total).astype(jnp.bfloat16)
    mixed = jnp.einsum(
        "inhqk,inkhe->inqhe", soft_weights, value_blocks, preferred_element_type=jnp.float32
    ).astype(jnp.bfloat16)
    mixed = mixed.reshape(image_count, ITOK, local_width)
    if reorder is not None:
        mixed = jnp.take(mixed, reorder[1], axis=1)
    mixed = mixed.reshape(image_count * ITOK, local_width)
    residual = hidden + branch_sum(mixed, w_proj) + norm_rows[2]
    ln_second, normed_second, inv_second = layer_norm(residual, norm_rows[3], norm_rows[4])
    spread = spread_rows(ln_second.astype(jnp.bfloat16))
    pre_active = jnp.dot(spread, w_fc1, preferred_element_type=jnp.float32) + b_fc1.astype(
        jnp.float32
    )
    active = gelu_value(pre_active).astype(jnp.bfloat16)
    result = residual + branch_sum(active, w_fc2) + norm_rows[5]
    kept_state = (
        normed_first,
        inv_first,
        permuted_rows,
        query_blocks,
        key_blocks,
        value_blocks,
        log_total,
        mixed,
        normed_second,
        inv_second,
        spread,
        pre_active,
        active,
    )
    return (result, kept_state)


def backward_layer(out_grad, kept_state, weights, lookup, mask_term, reorder):
    (
        normed_first,
        inv_first,
        permuted_rows,
        query_blocks,
        key_blocks,
        value_blocks,
        log_total,
        mixed,
        normed_second,
        inv_second,
        spread,
        pre_active,
        active,
    ) = kept_state
    w_qkv, b_qv, pos_table, w_proj, w_fc1, b_fc1, w_fc2, norm_rows = weights
    norm_rows = norm_rows.astype(jnp.float32)
    local_width = w_qkv.shape[-1]
    head_count = local_width // HEAD_DIM
    score_scale = HEAD_DIM ** (-0.5)
    image_count = permuted_rows.shape[0] // ITOK
    grad_rounded = spread_grads(out_grad.astype(jnp.bfloat16))
    d_fc2 = inner_rows(active, grad_rounded)
    d_active = times_transposed(grad_rounded, w_fc2)
    d_pre = d_active * gelu_slope(pre_active)
    d_bias_fc1 = jnp.sum(d_pre, axis=0)
    d_pre_rounded = d_pre.astype(jnp.bfloat16)
    d_fc1 = inner_rows(spread, d_pre_rounded)
    d_spread = back_sum(d_pre_rounded, w_fc1)
    d_residual = out_grad + norm_back(d_spread, normed_second, inv_second, norm_rows[3])
    mix_grad = spread_grads(d_residual.astype(jnp.bfloat16))
    d_proj = inner_rows(mixed, mix_grad)
    d_mixed = (
        times_transposed(mix_grad, w_proj)
        .astype(jnp.bfloat16)
        .reshape(image_count, ITOK, local_width)
    )
    if reorder is not None:
        d_mixed = jnp.take(d_mixed, reorder[0], axis=1)
    d_mixed_blocks = d_mixed.reshape(image_count, NWIN, WTOK, head_count, HEAD_DIM)
    pos_bias = position_bias(lookup, pos_table)
    scores = window_scores(query_blocks, key_blocks, pos_bias, mask_term)
    soft_exact = jnp.exp(scores - log_total)
    d_values = jnp.einsum(
        "inhqk,inqhe->inkhe",
        soft_exact.astype(jnp.bfloat16),
        d_mixed_blocks,
        preferred_element_type=jnp.float32,
    )
    d_soft = jnp.einsum(
        "inqhe,inkhe->inhqk", d_mixed_blocks, value_blocks, preferred_element_type=jnp.float32
    )
    d_scores = soft_exact * (d_soft - jnp.sum(soft_exact * d_soft, axis=-1, keepdims=True))
    score_total = jnp.sum(d_scores, axis=(0, 1)).reshape(head_count, WTOK * WTOK)
    d_table = jnp.dot(lookup.T, score_total.T, precision=full_precision)
    d_scores_rounded = d_scores.astype(jnp.bfloat16)
    d_query = (
        jnp.einsum(
            "inhqk,inkhe->inqhe", d_scores_rounded, key_blocks, preferred_element_type=jnp.float32
        )
        * score_scale
    )
    d_keys = jnp.einsum(
        "inhqk,inqhe->inkhe", d_scores_rounded, query_blocks, preferred_element_type=jnp.float32
    )
    d_query = d_query.reshape(-1, local_width)
    d_keys = d_keys.reshape(-1, local_width)
    d_values = d_values.reshape(-1, local_width)
    d_bias_qv = jnp.stack([jnp.sum(d_query, axis=0), jnp.sum(d_values, axis=0)])
    d_joint = (
        jnp.stack([d_query, d_keys, d_values], axis=1)
        .astype(jnp.bfloat16)
        .reshape(-1, 3 * local_width)
    )
    d_qkv = inner_rows(permuted_rows, d_joint).reshape(D, 3, local_width)
    if reorder is not None:
        d_joint = jnp.take(
            d_joint.reshape(image_count, ITOK, 3 * local_width), reorder[1], axis=1
        ).reshape(image_count * ITOK, 3 * local_width)
    d_normed = back_sum(d_joint, w_qkv.reshape(D, 3 * local_width))
    d_hidden = d_residual + norm_back(d_normed, normed_first, inv_first, norm_rows[0])
    norm_grads = jnp.stack(
        [
            jnp.sum(d_normed * normed_first, axis=0),
            jnp.sum(d_normed, axis=0),
            jnp.sum(d_residual, axis=0),
            jnp.sum(d_spread * normed_second, axis=0),
            jnp.sum(d_spread, axis=0),
            jnp.sum(out_grad, axis=0),
        ]
    )
    return (d_hidden, (d_qkv, d_proj, d_fc1, d_fc2), (d_bias_qv, d_table, d_bias_fc1), norm_grads)


def join_two(first_item, second_item):
    return jnp.concatenate([first_item, second_item], axis=0)


def body(
    block_input,
    cotangent,
    w_qkv,
    b_qv,
    bias_table,
    w_proj,
    w_fc1,
    b_fc1,
    w_fc2,
    norm_params,
    rel_index,
    shift_perm,
    shift_mask,
):
    full_qkv, full_proj, full_fc1, full_fc2, norm_rows = (
        lax.all_gather(w_qkv, "dp", axis=1, tiled=True),
        lax.all_gather(w_proj, "dp", axis=2, tiled=True),
        lax.all_gather(w_fc1, "dp", axis=1, tiled=True),
        lax.all_gather(w_fc2, "dp", axis=2, tiled=True),
        lax.all_gather(norm_params, "dp", axis=2, tiled=True),
    )
    head_bias, pos_table, fc1_bias = (b_qv, bias_table, b_fc1)
    inverse = jnp.zeros((ITOK,), jnp.int32).at[shift_perm].set(jnp.arange(ITOK, dtype=jnp.int32))
    reorder = (shift_perm, inverse)
    lookup = rel_lookup(rel_index)
    mask_term = shift_mask.astype(jnp.float32) * MASKED

    def weights_of(layer_index):
        return (
            full_qkv[layer_index],
            head_bias[layer_index],
            pos_table[layer_index],
            full_proj[layer_index],
            full_fc1[layer_index],
            fc1_bias[layer_index],
            full_fc2[layer_index],
            norm_rows[layer_index],
        )

    first_out, kept_first = forward_layer(block_input, weights_of(0), lookup, None, None)
    second_out, kept_second = forward_layer(first_out, weights_of(1), lookup, mask_term, reorder)
    kept_layers = (kept_first, kept_second)
    layer_masks = (None, mask_term)
    layer_orders = (None, reorder)
    grad_now = cotangent
    finished = []
    for layer_index in (1, 0):
        grad_now, weight_grads, small_grads, norm_grads = backward_layer(
            grad_now,
            kept_layers[layer_index],
            weights_of(layer_index),
            lookup,
            layer_masks[layer_index],
            layer_orders[layer_index],
        )
        d_qkv, d_proj, d_fc1, d_fc2 = weight_grads
        d_bias_qv, d_table, d_bias_fc1 = small_grads
        norm_sum = lax.psum(norm_grads, "tensor")
        shards = (d_qkv[None], d_proj[None], d_fc1[None], d_fc2[None], norm_sum[None])
        finished.append((shards, (d_bias_qv[None], d_table[None], d_bias_fc1[None])))
    later_layer = finished[0]
    earlier_layer = finished[1]
    joined_qkv, joined_proj, joined_fc1, joined_fc2, joined_norms = jax.tree.map(
        join_two, earlier_layer[0], later_layer[0]
    )
    small_qv, small_table, small_fc1 = jax.tree.map(join_two, earlier_layer[1], later_layer[1])
    joined_qkv, joined_proj, joined_fc1, joined_fc2, joined_norms = (
        lax.psum_scatter(
            joined_qkv.astype(jnp.bfloat16), "dp", scatter_dimension=1, tiled=True
        ).astype(jnp.float32),
        lax.psum_scatter(
            joined_proj.astype(jnp.bfloat16), "dp", scatter_dimension=2, tiled=True
        ).astype(jnp.float32),
        lax.psum_scatter(
            joined_fc1.astype(jnp.bfloat16), "dp", scatter_dimension=1, tiled=True
        ).astype(jnp.float32),
        lax.psum_scatter(
            joined_fc2.astype(jnp.bfloat16), "dp", scatter_dimension=2, tiled=True
        ).astype(jnp.float32),
        lax.psum_scatter(
            joined_norms.astype(jnp.bfloat16), "dp", scatter_dimension=2, tiled=True
        ).astype(jnp.float32),
    )
    d_bias_qv, d_table, d_bias_fc1 = lax.psum((small_qv, small_table, small_fc1), "dp")
    return (
        second_out,
        grad_now,
        joined_qkv,
        d_bias_qv,
        d_table,
        joined_proj,
        joined_fc1,
        d_bias_fc1,
        joined_fc2,
        joined_norms,
    )


def solution(mesh):
    in_specs = (
        P(("dp", "tensor"), None),
        P(("dp", "tensor"), None),
        P(None, "dp", None, "tensor"),
        P(None, None, "tensor"),
        P(None, None, "tensor"),
        P(None, "tensor", "dp"),
        P(None, "dp", "tensor"),
        P(None, "tensor"),
        P(None, "tensor", "dp"),
        P(None, None, "dp"),
        P(),
        P(),
        P(),
    )
    out_specs = (
        P(("dp", "tensor"), None),
        P(("dp", "tensor"), None),
        P(None, "dp", None, "tensor"),
        P(None, None, "tensor"),
        P(None, None, "tensor"),
        P(None, "tensor", "dp"),
        P(None, "dp", "tensor"),
        P(None, "tensor"),
        P(None, "tensor", "dp"),
        P(None, None, "dp"),
    )
    return jax.shard_map(body, mesh=mesh, in_specs=in_specs, out_specs=out_specs, check_vma=False)
```

profile of v0, /device:TPU:0, one launch (start us, length us, event | category | flops | bytes accessed | tf_op | source)
XLA Modules:
  0.0 1039.6 jit_solution(14769519194201761679)
XLA Ops:
  22.8 11.3 %slice_reduce_fusion.6 = (f32[512]{0:T(512)S(1)}, f32[512]{0:T(512)S(1)}, f32[512]{0:T(512)S(1)}, f32[512]{0:T(512)S(1)}, f32[512]{0:T(512)S(1)}, /*index=5*/f32[512]{0:T(512)S(1)}) fusion(f32[1,6,512]{1,0,2:T(1,128)S(1)} %get-tuple-element.115), kind=kLoop, calls=%fused_computation.203 | loop fusion | bytes 24576 | tf_op jit(solution)/shard_map/slice | solution.py:153
  58.8 14.3 %all-gather.11.cloned.1.call-done = bf16[1568,512]{1,0:T(8,128)(2,1)} async-done(((bf16[392,512]{1,0:T(8,128)(2,1)}), bf16[1568,512]{1,0:T(8,128)(2,1)}) %all-gather.11.cloned.1.call-update) | async-done | bytes 1605648 | tf_op jit(solution)/shard_map/all_gather | solution.py:84
  108.5 34.3 %reduce-scatter.14.cloned.1.call-done = bf16[392,512]{1,0:T(8,128)(2,1)} async-done(((bf16[1568,512]{1,0:T(8,128)(2,1)}), bf16[392,512]{1,0:T(8,128)(2,1)}) %reduce-scatter.14.cloned.1.call-update) | async-done | bytes 401424 | tf_op jit(solution)/shard_map/reduce_scatter | solution.py:92
  146.5 35.2 %all-gather.13.cloned.1.call-done = bf16[1568,512]{1,0:T(8,128)(2,1)} async-done(((bf16[392,512]{1,0:T(8,128)(2,1)}), bf16[1568,512]{1,0:T(8,128)(2,1)}) %all-gather.13.cloned.1.call-update) | async-done | bytes 1605648 | tf_op jit(solution)/shard_map/all_gather | solution.py:84
  186.2 19.4 %all-gather.17.cloned.1.call-done = bf16[2,512,512]{1,2,0:T(8,128)(2,1)} async-done(((bf16[2,512,64]{1,2,0:T(8,128)(2,1)}), bf16[2,512,512]{1,2,0:T(8,128)(2,1)}) %all-gather.17.cloned.1.call-update) | async-done | bytes 1048592 | tf_op jit(solution)/shard_map/all_gather | solution.py:290
  209.3 11.7 %slice_reduce_fusion = (f32[512]{0:T(512)}, f32[512]{0:T(512)}, f32[512]{0:T(512)}, f32[512]{0:T(512)}, f32[512]{0:T(512)S(1)}, /*index=5*/f32[512]{0:T(512)S(1)}) fusion(f32[1,6,512]{1,0,2:T(1,128)S(1)} %get-tuple-element.116), kind=kLoop, calls=%fused_computation.196 | loop fusion | bytes 24576 | tf_op jit(solution)/shard_map/slice | solution.py:153
  221.1 23.9 %reduce-scatter.16.cloned.1.call-done = bf16[392,512]{1,0:T(8,128)(2,1)} async-done(((bf16[1568,512]{1,0:T(8,128)(2,1)}), bf16[392,512]{1,0:T(8,128)(2,1)}) %reduce-scatter.16.cloned.1.call-update) | async-done | bytes 401424 | tf_op jit(solution)/shard_map/reduce_scatter | solution.py:92
  254.3 29.5 %all-gather.19.cloned.1.call-done = bf16[1568,512]{1,0:T(8,128)(2,1)} async-done(((bf16[392,512]{1,0:T(8,128)(2,1)}), bf16[1568,512]{1,0:T(8,128)(2,1)}) %all-gather.19.cloned.1.call-update) | async-done | bytes 1605648 | tf_op jit(solution)/shard_map/all_gather | solution.py:84
  343.9 34.9 %reduce-scatter.18.cloned.1.call-done = bf16[392,512]{1,0:T(8,128)(2,1)} async-done(((bf16[1568,512]{1,0:T(8,128)(2,1)}), bf16[392,512]{1,0:T(8,128)(2,1)}) %reduce-scatter.18.cloned.1.call-update) | async-done | bytes 401424 | tf_op jit(solution)/shard_map/reduce_scatter | solution.py:92
  385.4 35.5 %all-gather.21.cloned.1.call-done = bf16[1568,512]{1,0:T(8,128)(2,1)} async-done(((bf16[392,512]{1,0:T(8,128)(2,1)}), bf16[1568,512]{1,0:T(8,128)(2,1)}) %all-gather.21.cloned.1.call-update) | async-done | bytes 1605648 | tf_op jit(solution)/shard_map/all_gather | solution.py:84
  426.1 33.3 %all-gather.23.cloned.1.call-done = bf16[1568,512]{1,0:T(8,128)(2,1)} async-done(((bf16[392,512]{1,0:T(8,128)(2,1)}), bf16[1568,512]{1,0:T(8,128)(2,1)}) %all-gather.23.cloned.1.call-update) | async-done | bytes 1605648 | tf_op jit(solution)/shard_map/all_gather | solution.py:88
  471.9 31.0 %reduce-scatter.22.cloned.1.call-done = bf16[392,512]{1,0:T(8,128)(2,1)} async-done(((bf16[1568,512]{1,0:T(8,128)(2,1)}), bf16[392,512]{1,0:T(8,128)(2,1)}) %reduce-scatter.22.cloned.1.call-update) | async-done | bytes 401424 | tf_op jit(solution)/shard_map/reduce_scatter | solution.py:101
  506.1 33.7 %reduce-scatter.20.cloned.1.call-done = bf16[392,512]{1,0:T(8,128)(2,1)} async-done(((bf16[1568,512]{1,0:T(8,128)(2,1)}), bf16[392,512]{1,0:T(8,128)(2,1)}) %reduce-scatter.20.cloned.1.call-update) | async-done | bytes 401424 | tf_op jit(solution)/shard_map/reduce_scatter | solution.py:92
  544.9 36.5 %all-gather.25.cloned.1.call-done = bf16[1568,512]{1,0:T(8,128)(2,1)} async-done(((bf16[392,512]{1,0:T(8,128)(2,1)}), bf16[1568,512]{1,0:T(8,128)(2,1)}) %all-gather.25.cloned.1.call-update) | async-done | bytes 1605648 | tf_op jit(solution)/shard_map/all_gather | solution.py:88
  641.7 34.9 %reduce-scatter.24.cloned.1.call-done = bf16[392,512]{1,0:T(8,128)(2,1)} async-done(((bf16[1568,512]{1,0:T(8,128)(2,1)}), bf16[392,512]{1,0:T(8,128)(2,1)}) %reduce-scatter.24.cloned.1.call-update) | async-done | bytes 401424 | tf_op jit(solution)/shard_map/reduce_scatter | solution.py:101
  682.4 36.3 %all-gather.27.cloned.1.call-done = bf16[1568,512]{1,0:T(8,128)(2,1)} async-done(((bf16[392,512]{1,0:T(8,128)(2,1)}), bf16[1568,512]{1,0:T(8,128)(2,1)}) %all-gather.27.cloned.1.call-update) | async-done | bytes 1605648 | tf_op jit(solution)/shard_map/all_gather | solution.py:88
  727.4 34.9 %reduce-scatter.26.cloned.1.call-done = bf16[392,512]{1,0:T(8,128)(2,1)} async-done(((bf16[1568,512]{1,0:T(8,128)(2,1)}), bf16[392,512]{1,0:T(8,128)(2,1)}) %reduce-scatter.26.cloned.1.call-update) | async-done | bytes 401424 | tf_op jit(solution)/shard_map/reduce_scatter | solution.py:101
  784.4 20.1 %all-gather.29.cloned.1.call-done = bf16[1568,512]{1,0:T(8,128)(2,1)} async-done(((bf16[392,512]{1,0:T(8,128)(2,1)}), bf16[1568,512]{1,0:T(8,128)(2,1)}) %all-gather.29.cloned.1.call-update) | async-done | bytes 1605648 | tf_op jit(solution)/shard_map/all_gather | solution.py:88
  855.5 23.5 %all-reduce.2 = (f32[2,2,128]{2,1,0:T(2,128)}, f32[2,169,4]{1,2,0:T(4,128)}, f32[2,512]{1,0:T(2,128)}) all-reduce(f32[2,2,128]{2,1,0:T(2,128)S(1)} %pad_maximum_fusion.7, f32[2,169,4]{1,2,0:T(4,128)S(1)} %pad_maximum_fusion.5, f32[2,512]{1,0:T(2,128)S(1)} %pad_maximum_fusion.6), channel_id=1, replica_groups=mesh['dp'=8,'tensor'=4] {'dp'}, use_global_device_ids=true, to_apply=%region_36.38 | all-reduce | flops 2888 | bytes 23104 | tf_op jit(solution)/shard_map/psum | solution.py:355
  879.1 24.1 %all-reduce.7.cloned.1.call-done = (bf16[2,128,512]{1,0,2:T(2,128)(2,1)}, bf16[2,512,512]{1,0,2:T(2,128)(2,1)}) async-done(((bf16[2,128,512]{1,0,2:T(2,128)(2,1)}, bf16[2,512,512]{1,0,2:T(2,128)(2,1)}), (bf16[2,128,512]{1,0,2:T(2,128)(2,1)}, bf16[2,512,512]{1,0,2:T(2,128)(2,1)})) %all-reduce.7.cloned.1.call-update) | async-done | bytes 1310736
  906.4 34.0 %reduce-scatter.30.cloned.1.call-done = bf16[2,64,3,128]{3,1,2,0:T(8,128)(2,1)} async-done(((bf16[2,512,3,128]{3,1,2,0:T(8,128)(2,1)}), bf16[2,64,3,128]{3,1,2,0:T(8,128)(2,1)}) %reduce-scatter.30.cloned.1.call-update) | async-done | bytes 98320 | tf_op jit(solution)/shard_map/reduce_scatter | solution.py:339
  942.0 36.5 %reduce-scatter.28.cloned.1.call-done = bf16[392,512]{1,0:T(8,128)(2,1)} async-done(((bf16[1568,512]{1,0:T(8,128)(2,1)}), bf16[392,512]{1,0:T(8,128)(2,1)}) %reduce-scatter.28.cloned.1.call-update) | async-done | bytes 401424 | tf_op jit(solution)/shard_map/reduce_scatter | solution.py:101
  980.2 17.0 %all-reduce.3 = (bf16[6,512]{1,0:T(8,128)(2,1)S(1)}, bf16[6,512]{1,0:T(8,128)(2,1)S(1)}) all-reduce(f32[6,512]{1,0:T(8,128)S(1)} %stack.87, f32[6,512]{1,0:T(8,128)S(1)} %stack.80), channel_id=1, replica_groups=mesh['dp'=8,'tensor'=4] {'tensor'}, use_global_device_ids=true, to_apply=%region_59.61 | all-reduce | flops 6144 | bytes 36864 | tf_op jit(solution)/shard_map/psum | solution.py:329
  999.4 30.8 %reduce-scatter.34.cloned.1.call-done = bf16[64,12]{1,0:T(8,128)(2,1)} async-done(((bf16[512,12]{1,0:T(8,128)(2,1)}), bf16[64,12]{1,0:T(8,128)(2,1)}) %reduce-scatter.34.cloned.1.call-update) | async-done | bytes 1552
  (473 shorter events, 344.5 us)
Async XLA Ops:
  8.0 65.1 %all-gather.11.cloned.1.call-start = ((), (), s32[]{:S(2)}) async-start(), calls=%async_computation.11 | async-start | bytes 2007040 | tf_op jit(solution)/shard_map/all_gather | solution.py:84
  35.1 107.8 %reduce-scatter.14.cloned.1.call-start = ((), (), s32[]{:S(2)}) async-start(), calls=%async_computation.12 | async-start | bytes 2007040 | tf_op jit(solution)/shard_map/reduce_scatter | solution.py:92
  107.9 38.6 %all-gather.15.cloned.1.call-start = ((), (), s32[]{:S(2)}) async-start(), calls=%async_computation.14 | async-start | bytes 1179648 | tf_op jit(solution)/shard_map/all_gather | solution.py:289
  108.4 73.2 %all-gather.13.cloned.1.call-start = ((), (), s32[]{:S(2)}) async-start(), calls=%async_computation.13 | async-start | bytes 2007040 | tf_op jit(solution)/shard_map/all_gather | solution.py:84
  145.3 60.3 %all-gather.17.cloned.1.call-start = ((), (), s32[]{:S(2)}) async-start(), calls=%async_computation.15 | async-start | bytes 1179648 | tf_op jit(solution)/shard_map/all_gather | solution.py:290
  145.9 99.1 %reduce-scatter.16.cloned.1.call-start = ((), (), s32[]{:S(2)}) async-start(), calls=%async_computation.16 | async-start | bytes 2007040 | tf_op jit(solution)/shard_map/reduce_scatter | solution.py:92
  208.9 75.0 %all-gather.19.cloned.1.call-start = ((), (), s32[]{:S(2)}) async-start(), calls=%async_computation.17 | async-start | bytes 2007040 | tf_op jit(solution)/shard_map/all_gather | solution.py:84
  247.5 131.3 %reduce-scatter.18.cloned.1.call-start = ((), (), s32[]{:S(2)}) async-start(), calls=%async_computation.18 | async-start | bytes 2007040 | tf_op jit(solution)/shard_map/reduce_scatter | solution.py:92
  343.9 77.0 %all-gather.21.cloned.1.call-start = ((), (), s32[]{:S(2)}) async-start(), calls=%async_computation.19 | async-start | bytes 2007040 | tf_op jit(solution)/shard_map/all_gather | solution.py:84
  384.4 75.0 %all-gather.23.cloned.1.call-start = ((), (), s32[]{:S(2)}) async-start(), calls=%async_computation.21 | async-start | bytes 2007040 | tf_op jit(solution)/shard_map/all_gather | solution.py:88
  384.9 117.9 %reduce-scatter.22.cloned.1.call-start = ((), (), s32[]{:S(2)}) async-start(), calls=%async_computation.22 | async-start | bytes 2007040 | tf_op jit(solution)/shard_map/reduce_scatter | solution.py:101
  468.0 71.9 %reduce-scatter.20.cloned.1.call-start = ((), (), s32[]{:S(2)}) async-start(), calls=%async_computation.20 | async-start | bytes 2007040 | tf_op jit(solution)/shard_map/reduce_scatter | solution.py:92
  471.8 109.5 %all-gather.25.cloned.1.call-start = ((), (), s32[]{:S(2)}) async-start(), calls=%async_computation.23 | async-start | bytes 2007040 | tf_op jit(solution)/shard_map/all_gather | solution.py:88
  544.8 131.8 %reduce-scatter.24.cloned.1.call-start = ((), (), s32[]{:S(2)}) async-start(), calls=%async_computation.24 | async-start | bytes 2007040 | tf_op jit(solution)/shard_map/reduce_scatter | solution.py:101
  641.7 77.1 %all-gather.27.cloned.1.call-start = ((), (), s32[]{:S(2)}) async-start(), calls=%async_computation.25 | async-start | bytes 2007040 | tf_op jit(solution)/shard_map/all_gather | solution.py:88
  682.3 80.0 %reduce-scatter.26.cloned.1.call-start = ((), (), s32[]{:S(2)}) async-start(), calls=%async_computation.26 | async-start | bytes 2007040 | tf_op jit(solution)/shard_map/reduce_scatter | solution.py:101
  727.4 77.1 %all-gather.29.cloned.1.call-start = ((), (), s32[]{:S(2)}) async-start(), calls=%async_computation.27 | async-start | bytes 2007040 | tf_op jit(solution)/shard_map/all_gather | solution.py:88
  768.1 84.5 %reduce-scatter.32.cloned.1.call-start = ((), (), s32[]{:S(2)}) async-start(), calls=%async_computation.30 | async-start | bytes 1179648 | tf_op jit(solution)/shard_map/reduce_scatter | solution.py:345
  784.4 118.9 %all-reduce.7.cloned.1.call-start = ((), (), s32[]{:S(2)}) async-start(), calls=%async_computation.32 | async-start | bytes 2621440
  842.0 98.4 %reduce-scatter.30.cloned.1.call-start = ((), (), s32[]{:S(2)}) async-start(), calls=%async_computation.29 | async-start | bytes 884736 | tf_op jit(solution)/shard_map/reduce_scatter | solution.py:339
  845.8 132.8 %reduce-scatter.28.cloned.1.call-start = ((), (), s32[]{:S(2)}) async-start(), calls=%async_computation.28 | async-start | bytes 2007040 | tf_op jit(solution)/shard_map/reduce_scatter | solution.py:101
  849.6 129.0 %copy-start.64 = (f32[512]{0:T(512)S(1)}, f32[512]{0:T(512)}, u32[]{:S(2)}) copy-start(f32[512]{0:T(512)} %copy-done.63) | copy-start | bytes 6148
  849.6 180.7 %reduce-scatter.34.cloned.1.call-start = ((), (), s32[]{:S(2)}) async-start(), calls=%async_computation.31 | async-start | bytes 147456
  854.6 143.6 %copy-start.20 = (f32[392,512]{1,0:T(8,128)S(1)}, f32[392,512]{1,0:T(8,128)}, u32[]{:S(2)}) copy-start(f32[392,512]{1,0:T(8,128)} %copy-done.19) | copy-start | bytes 2408452
  (106 other events, 1835.2 us)
Sparse Core Ops, SparseCore 0:
  35.2 37.8 all-gather.10
  108.0 34.7 reduce-scatter.13
  209.0 35.9 reduce-scatter.15
  384.5 36.3 all-gather.20
  422.9 36.4 all-gather.22
  544.9 36.3 all-gather.24
  641.8 34.7 reduce-scatter.23
  727.5 34.8 reduce-scatter.25
Sparse Core Ops, SparseCore 1:
  110.3 22.1 all-gather.14
  145.4 36.2 all-gather.12
  183.5 22.1 all-gather.16
  247.6 36.2 all-gather.18
  344.0 34.8 reduce-scatter.17
  468.0 34.8 reduce-scatter.21
  505.0 34.7 reduce-scatter.19
  682.4 36.2 all-gather.26
  768.2 36.3 all-gather.28
  807.7 34.8 reduce-scatter.31
  845.6 57.5 all-reduce.6
  906.4 34.0 reduce-scatter.29
  942.6 35.9 reduce-scatter.27
  998.3 31.9 reduce-scatter.33
where the time goes:
time: 1050 us; the launch traced here: 1040 us
  waiting for transfers between devices  615 us (59%)
  local copies, waits for them, and re-layouts  177 us (17%)
  matrix products  95.6 us (9%)
  blocking collectives  70.2 us (7%)
  other arithmetic  61.5 us (6%)
  between operations  18.3 us (2%)
    reduce_scatter x4, waiting for transfers between devices, back_sum(): lax.psum_scatter(times_transposed(values, weight).astype(jnp.bfloat16), '...  137 us
    reduce_scatter x4, waiting for transfers between devices, branch_sum(): lax.psum_scatter(jnp.dot(values, weight, preferred_element_type=jnp.float...  127 us
    all_gather x4, waiting for transfers between devices, spread_grads(): return lax.all_gather(values, 'tensor', axis=0, tiled=True)  126 us
    all_gather x4, waiting for transfers between devices, spread_rows(): return lax.all_gather(values, 'tensor', axis=0, tiled=True)  114 us
    unnamed x24, waiting for transfers between devices  56.8 us
    reduce_scatter x1, waiting for transfers between devices, body(): lax.psum_scatter(joined_qkv.astype(jnp.bfloat16), 'dp', scatter_dimension...  34 us
    dot_general x8, matrix products, times_transposed(): lax.dot_general(left_side, right_side, (((1,), (1,)), ((), ())), preferre...  25.2 us
    psum x1, blocking collectives, body(): lax.psum((small_qv, small_table, small_fc1), 'dp')  23.5 us
  transfers between devices with their start and end apart: 22, of which 20 were waited for; matrix products, arithmetic and copies ran while one was open for 11% of the time, Pallas kernels for 0%

commit v1 on v0

--- a/solution.py
+++ b/solution.py
@@ -81,29 +81,65 @@
 
 
 def spread_rows(values):
-    return lax.all_gather(values, "tensor", axis=0, tiled=True)
+    return values
 
 
 def spread_grads(values):
-    return lax.all_gather(values, "tensor", axis=0, tiled=True)
+    return values
 
 
 def branch_sum(values, weight):
-    return lax.psum_scatter(
-        jnp.dot(values, weight, preferred_element_type=jnp.float32).astype(jnp.bfloat16),
-        "tensor",
-        scatter_dimension=0,
-        tiled=True,
-    ).astype(jnp.float32)
+    return jnp.dot(values, weight, preferred_element_type=jnp.float32)
 
 
 def back_sum(values, weight):
-    return lax.psum_scatter(
-        times_transposed(values, weight).astype(jnp.bfloat16),
-        "tensor",
-        scatter_dimension=0,
-        tiled=True,
-    ).astype(jnp.float32)
+    return times_transposed(values, weight)
+
+
+def gather_both(shard, dp_dim, tensor_dim):
+    gathered = lax.all_gather(shard, ("dp", "tensor"), axis=0, tiled=False)
+    return join_blocks(gathered, dp_dim, tensor_dim)
+
+
+def join_blocks(gathered, dp_dim, tensor_dim):
+    n_dp, n_tensor = lax.axis_size("dp"), lax.axis_size("tensor")
+    shape = gathered.shape[1:]
+    blocks = gathered.reshape((n_dp, n_tensor) + shape)
+    order = []
+    final = []
+    for dim, size in enumerate(shape):
+        if dim == dp_dim:
+            order.append(0)
+            size *= n_dp
+        if dim == tensor_dim:
+            order.append(1)
+            size *= n_tensor
+        order.append(dim + 2)
+        final.append(size)
+    return blocks.transpose(order).reshape(final)
+
+
+def scatter_both(grads, dp_dim, tensor_dim):
+    n_dp, n_tensor = lax.axis_size("dp"), lax.axis_size("tensor")
+    split = []
+    front = [None, None]
+    rest = []
+    for dim, size in enumerate(grads.shape):
+        if dim == dp_dim:
+            front[0] = len(split)
+            split.append(n_dp)
+            size //= n_dp
+        if dim == tensor_dim:
+            front[1] = len(split)
+            split.append(n_tensor)
+            size //= n_tensor
+        rest.append(len(split))
+        split.append(size)
+    blocks = grads.astype(jnp.bfloat16).reshape(split).transpose(front + rest)
+    shape = blocks.shape[2:]
+    part = lax.psum_scatter(blocks, "dp", scatter_dimension=0, tiled=False)
+    part = lax.psum_scatter(part, "tensor", scatter_dimension=0, tiled=False)
+    return part.reshape(shape).astype(jnp.float32)
 
 
 def forward_layer(hidden, weights, lookup, mask_term, reorder):
@@ -283,14 +319,16 @@
     shift_perm,
     shift_mask,
 ):
-    full_qkv, full_proj, full_fc1, full_fc2, norm_rows = (
-        lax.all_gather(w_qkv, "dp", axis=1, tiled=True),
-        lax.all_gather(w_proj, "dp", axis=2, tiled=True),
-        lax.all_gather(w_fc1, "dp", axis=1, tiled=True),
-        lax.all_gather(w_fc2, "dp", axis=2, tiled=True),
-        lax.all_gather(norm_params, "dp", axis=2, tiled=True),
-    )
-    head_bias, pos_table, fc1_bias = (b_qv, bias_table, b_fc1)
+    full_qkv, full_proj, full_fc1, full_fc2 = (
+        gather_both(w_qkv, 1, 3),
+        gather_both(w_proj, 2, 1),
+        gather_both(w_fc1, 1, 2),
+        gather_both(w_fc2, 2, 1),
+    )
+    norm_rows = lax.all_gather(norm_params, "dp", axis=2, tiled=True)
+    head_bias = lax.all_gather(b_qv, "tensor", axis=2, tiled=True)
+    pos_table = lax.all_gather(bias_table, "tensor", axis=2, tiled=True)
+    fc1_bias = lax.all_gather(b_fc1, "tensor", axis=1, tiled=True)
     inverse = jnp.zeros((ITOK,), jnp.int32).at[shift_perm].set(jnp.arange(ITOK, dtype=jnp.int32))
     reorder = (shift_perm, inverse)
     lookup = rel_lookup(rel_index)
@@ -326,33 +364,30 @@
         )
         d_qkv, d_proj, d_fc1, d_fc2 = weight_grads
         d_bias_qv, d_table, d_bias_fc1 = small_grads
-        norm_sum = lax.psum(norm_grads, "tensor")
-        shards = (d_qkv[None], d_proj[None], d_fc1[None], d_fc2[None], norm_sum[None])
-        finished.append((shards, (d_bias_qv[None], d_table[None], d_bias_fc1[None])))
+        shards = (d_qkv[None], d_proj[None], d_fc1[None], d_fc2[None])
+        finished.append((shards, (d_bias_qv[None], d_table[None], d_bias_fc1[None], norm_grads[None])))
     later_layer = finished[0]
     earlier_layer = finished[1]
-    joined_qkv, joined_proj, joined_fc1, joined_fc2, joined_norms = jax.tree.map(
+    joined_qkv, joined_proj, joined_fc1, joined_fc2 = jax.tree.map(
         join_two, earlier_layer[0], later_layer[0]
     )
-    small_qv, small_table, small_fc1 = jax.tree.map(join_two, earlier_layer[1], later_layer[1])
-    joined_qkv, joined_proj, joined_fc1, joined_fc2, joined_norms = (
-        lax.psum_scatter(
-            joined_qkv.astype(jnp.bfloat16), "dp", scatter_dimension=1, tiled=True
-        ).astype(jnp.float32),
-        lax.psum_scatter(
-            joined_proj.astype(jnp.bfloat16), "dp", scatter_dimension=2, tiled=True
-        ).astype(jnp.float32),
-        lax.psum_scatter(
-            joined_fc1.astype(jnp.bfloat16), "dp", scatter_dimension=1, tiled=True
-        ).astype(jnp.float32),
-        lax.psum_scatter(
-            joined_fc2.astype(jnp.bfloat16), "dp", scatter_dimension=2, tiled=True
-        ).astype(jnp.float32),
-        lax.psum_scatter(
-            joined_norms.astype(jnp.bfloat16), "dp", scatter_dimension=2, tiled=True
-        ).astype(jnp.float32),
-    )
-    d_bias_qv, d_table, d_bias_fc1 = lax.psum((small_qv, small_table, small_fc1), "dp")
+    smalls = jax.tree.map(join_two, earlier_layer[1], later_layer[1])
+    joined_qkv, joined_proj, joined_fc1, joined_fc2 = (
+        scatter_both(joined_qkv, 1, 3),
+        scatter_both(joined_proj, 2, 1),
+        scatter_both(joined_fc1, 1, 2),
+        scatter_both(joined_fc2, 2, 1),
+    )
+    small_qv, small_table, small_fc1, small_norms = lax.psum(smalls, ("dp", "tensor"))
+    dp_at, tensor_at = lax.axis_index("dp"), lax.axis_index("tensor")
+
+    def own_part(values, at, size, dim):
+        return lax.dynamic_slice_in_dim(values, at * size, size, axis=dim)
+
+    d_bias_qv = own_part(small_qv, tensor_at, b_qv.shape[2], 2)
+    d_table = own_part(small_table, tensor_at, bias_table.shape[2], 2)
+    d_bias_fc1 = own_part(small_fc1, tensor_at, b_fc1.shape[1], 1)
+    joined_norms = own_part(small_norms, dp_at, norm_params.shape[2], 2)
     return (
         second_out,
         grad_now,

time: 1050 us -> 897 us (0.85)
  waiting for transfers between devices: 615 us -> 441 us
  local copies, waits for them, and re-layouts: 177 us -> 253 us
  blocking collectives: 70.2 us -> 47.5 us
  matrix products: 95.6 us -> 79.2 us
    all_gather x10 -> x4, waiting for transfers between devices: 260 us -> 106 us  [gather_both(): gathered = lax.all_gather(shard, ('dp', 'tensor'), axis=0, tiled=False)]
    reduce_scatter x10 -> x4, waiting for transfers between devices: 298 us -> 144 us  [the longest x2 104 us: scatter_both(): part = lax.psum_scatter(blocks, 'dp', scatter_dimension=0, tiled=False)]
    psum x0 -> x1, waiting for transfers between devices: none -> 127 us  [body(): lax.psum(smalls, ('dp', 'tensor'))]
    psum x2 -> x0, blocking collectives: 40.5 us -> none  [the longest x1 23.5 us: body(): lax.psum((small_qv, small_table, small_fc1), 'dp')]
    reshape x0 -> x6, local copies, waits for them, and re-layouts: none -> 19.7 us  [the longest x4 18.1 us: join_blocks(): blocks = gathered.reshape((n_dp, n_tensor) + shape)]
    all_gather x3 -> x4, blocking collectives: 29.7 us -> 47.5 us  [the longest x1 13.2 us: body(): pos_table = lax.all_gather(bias_table, 'tensor', axis=2, tiled=True)]
    another operation x6 -> x12, local copies, waits for them, and re-layouts: 18.2 us -> 34.2 us  [backward_layer(): jnp.stack([d_query, d_keys, d_values], axis=1).astype(jnp.bfloat16)]
    dot_general x0 -> x8, local copies, waits for them, and re-layouts: none -> 13.3 us  [the longest x6 8.85 us: inner_rows(): lax.dot_general(left_side, right_side, (((0,), (0,)), ((), ())), preferre...]
  transfers between devices with their start and end apart: 22 -> 11, of which waited for: 20 -> 10; matrix products, arithmetic and copies ran while one was open for 11% -> 18% of each run, Pallas kernels for 0% -> 0%
where the time goes in v1:
time: 897 us; the launch traced here: 891 us
  waiting for transfers between devices  441 us (49%)
  local copies, waits for them, and re-layouts  253 us (28%)
  matrix products  79.2 us (9%)
  other arithmetic  53.7 us (6%)
  blocking collectives  47.5 us (5%)
  between operations  15.8 us (2%)
    psum x1, waiting for transfers between devices, body(): lax.psum(smalls, ('dp', 'tensor'))  127 us
    all_gather x4, waiting for transfers between devices, gather_both(): gathered = lax.all_gather(shard, ('dp', 'tensor'), axis=0, tiled=False)  106 us
    reduce_scatter x2, waiting for transfers between devices, scatter_both(): part = lax.psum_scatter(blocks, 'dp', scatter_dimension=0, tiled=False)  104 us
    unnamed x13, waiting for transfers between devices  64 us
    reduce_scatter x2, waiting for transfers between devices, scatter_both(): part = lax.psum_scatter(part, 'tensor', scatter_dimension=0, tiled=False)  40.5 us
    another operation x12, local copies, waits for them, and re-layouts, backward_layer(): jnp.stack([d_query, d_keys, d_values], axis=1).astype(jnp.bfloat16)  34.2 us
    unnamed x225, local copies, waits for them, and re-layouts  23.3 us
    slice x1, local copies, waits for them, and re-layouts, forward_layer(): result = residual + branch_sum(active, w_fc2) + norm_rows[5]  21.4 us
  transfers between devices with their start and end apart: 11, of which 10 were waited for; matrix products, arithmetic and copies ran while one was open for 18% of the time, Pallas kernels for 0%

profile of v1, /device:TPU:0, one launch (start us, length us, event | category | flops | bytes accessed | tf_op | source)
XLA Modules:
  0.0 890.6 jit_solution(8534958322342594030)
XLA Ops:
  10.0 12.9 %all_gather.39 = bf16[2,2,512]{2,1,0:T(2,128)(2,1)S(1)} all-gather(bf16[2,2,128]{2,1,0:T(2,128)(2,1)} %param.18), channel_id=1, replica_groups=mesh['dp'=8,'tensor'=4] {'tensor'}, dimensions={2}, use_global_device_ids=true | all-gather | bytes 5120 | tf_op jit(solution)/shard_map/all_gather | solution.py:329
  25.8 13.2 %all_gather.40 = bf16[2,169,16]{1,0,2:T(2,128)(2,1)S(1)} all-gather(bf16[2,169,4]{1,0,2:T(2,128)(2,1)S(1)} %copy.368), channel_id=1, replica_groups=mesh['dp'=8,'tensor'=4] {'tensor'}, dimensions={2}, use_global_device_ids=true | all-gather | bytes 13520 | tf_op jit(solution)/shard_map/all_gather | solution.py:330
  43.4 9.3 %all_gather.36 = bf16[2,6,512]{1,0,2:T(2,128)(2,1)S(1)} all-gather(bf16[2,6,64]{1,0,2:T(2,128)(2,1)S(1)} %copy.360), channel_id=1, replica_groups=mesh['dp'=8,'tensor'=4] {'dp'}, dimensions={2}, use_global_device_ids=true | all-gather | bytes 13824 | tf_op jit(solution)/shard_map/all_gather | solution.py:328
  52.7 12.1 %all_gather.45 = bf16[2,2048]{1,0:T(2,128)(2,1)S(1)} all-gather(bf16[2,512]{1,0:T(2,128)(2,1)S(1)} %copy-done.98), channel_id=1, replica_groups=mesh['dp'=8,'tensor'=4] {'tensor'}, dimensions={1}, use_global_device_ids=true | all-gather | bytes 10240 | tf_op jit(solution)/shard_map/all_gather | solution.py:331
  67.2 21.4 %slice_reduce_fusion = (f32[512]{0:T(512)}, f32[512]{0:T(512)}, f32[512]{0:T(512)}, f32[512]{0:T(512)}, f32[512]{0:T(512)}, /*index=5*/f32[512]{0:T(512)S(1)}, f...) fusion(f32[1,6,512]{1,0,2:T(1,128)S(1)} %get-tuple-element.128, ...), kind=kLoop, calls=%fused_computation.174 | loop fusion | bytes 49152 | tf_op jit(solution)/shard_map/slice | solution.py:189
  92.8 35.8 %all-gather.9.cloned.1.call-done = bf16[64,64,3,128]{3,1,2,0:T(8,128)(2,1)} async-done(((bf16[2,64,3,128]{3,1,2,0:T(8,128)(2,1)}), bf16[64,64,3,128]{3,1,2,0:T(8,128)(2,1)}) %all-gather.9.cloned.1.call-update) | async-done | bytes 3145744 | tf_op jit(solution)/shard_map/all_gather | solution.py:100
  128.6 4.5 copy.568
  175.0 17.0 %all-gather.13.cloned.1.call-done = bf16[64,64,512]{2,1,0:T(8,128)(2,1)} async-done(((bf16[2,64,512]{2,1,0:T(8,128)(2,1)}), bf16[64,64,512]{2,1,0:T(8,128)(2,1)}) %all-gather.13.cloned.1.call-update) | async-done | bytes 4194320 | tf_op jit(solution)/shard_map/all_gather | solution.py:100
  192.0 5.7 copy.567
  202.4 52.9 %all-gather.15.cloned.1.call-done = bf16[64,512,64]{1,2,0:T(8,128)(2,1)} async-done(((bf16[2,512,64]{1,2,0:T(8,128)(2,1)}), bf16[64,512,64]{1,2,0:T(8,128)(2,1)}) %all-gather.15.cloned.1.call-update) | async-done | bytes 4194320 | tf_op jit(solution)/shard_map/all_gather | solution.py:100
  255.3 5.7 copy.566
  312.5 4.5 copy.458
  351.4 4.7 fusion.112
  395.0 5.7 gather_fusion
  423.5 4.2 fusion.114
  483.6 4.3 convolution_convert_fusion.1
  493.7 5.5 maximum_bitcast_fusion.1
  529.9 23.1 %all-reduce.13.cloned.1.call-done = (bf16[8,4,2,64,3,128]{5,3,1,4,0,2:T(8,128)(2,1)}, bf16[8,4,2,128,64]{3,4,0,1,2:T(8,128)(2,1)}) async-done(((bf16[8,4,2,64,3,128]{5,3,1,4,0,2:T(8,128)(2,1)}, bf16[8,4,2,128,64]{3,4,0,1,2:T(8,128)(2,1)}), (bf16[8,4,2,64,3,128]{5,3,1,4,0,2:T(8,128)(2,1)}, bf16[8,4,2,128,64]{3,4,0,1,2:T(8,128)(2,1)})) %all-reduce.13.cloned.1.call-update) | async-done | bytes 4194320
  557.8 49.7 %reduce-scatter.21.cloned.1.call-done = bf16[1,4,2,512,64]{3,4,2,1,0:T(8,128)(2,1)} async-done(((bf16[8,4,2,512,64]{3,4,2,1,0:T(8,128)(2,1)}), bf16[1,4,2,512,64]{3,4,2,1,0:T(8,128)(2,1)}) %reduce-scatter.21.cloned.1.call-update) | async-done | bytes 524304 | tf_op jit(solution)/shard_map/reduce_scatter | solution.py:140
  608.1 53.9 %reduce-scatter.17.cloned.1.call-done = bf16[1,4,2,64,512]{4,3,2,1,0:T(8,128)(2,1)} async-done(((bf16[8,4,2,64,512]{4,3,2,1,0:T(8,128)(2,1)}), bf16[1,4,2,64,512]{4,3,2,1,0:T(8,128)(2,1)}) %reduce-scatter.17.cloned.1.call-update) | async-done | bytes 524304 | tf_op jit(solution)/shard_map/reduce_scatter | solution.py:140
  665.4 126.9 %all-reduce.11.cloned.1.call-done = (f32[2,2,512]{2,1,0:T(2,128)}, f32[2,169,16]{1,2,0:T(8,128)}, f32[2,2048]{1,0:T(2,128)}, f32[2,6,512]{2,1,0:T(8,128)}) async-done(((f32[2,2,512]{2,1,0:T(2,128)}, f32[2,169,16]{1,2,0:T(8,128)}, f32[2,2048]{1,0:T(2,128)}, f32[2,6,512]{2,1,0:T(8,128)}), (f32[2,2,512]{2,1,0:T(2,128)}, f32[2,169,16]{1,2,0:T(8,128)}, f32[2,2048]{1,0:T(2,128)}, ...) | async-done | bytes 70800 | tf_op jit(solution)/shard_map/psum | solution.py:381
  797.6 38.2 %all-reduce.15.cloned.1.call-done = (bf16[4,2,64,3,128]{4,2,0,3,1:T(8,128)(2,1)}, bf16[4,2,128,64]{2,3,0,1:T(8,128)(2,1)}) async-done(((bf16[4,2,64,3,128]{4,2,0,3,1:T(8,128)(2,1)}, bf16[4,2,128,64]{2,3,0,1:T(8,128)(2,1)}), (bf16[4,2,64,3,128]{4,2,0,3,1:T(8,128)(2,1)}, bf16[4,2,128,64]{2,3,0,1:T(8,128)(2,1)})) %all-reduce.15.cloned.1.call-update) | async-done | bytes 524304
  839.8 19.8 %reduce-scatter.23.cloned.1.call-done = bf16[1,2,512,64]{2,3,1,0:T(8,128)(2,1)} async-done(((bf16[4,2,512,64]{2,3,1,0:T(8,128)(2,1)}), bf16[1,2,512,64]{2,3,1,0:T(8,128)(2,1)}) %reduce-scatter.23.cloned.1.call-update) | async-done | bytes 131088 | tf_op jit(solution)/shard_map/reduce_scatter | solution.py:141
  861.2 20.8 %reduce-scatter.19.cloned.1.call-done = bf16[1,2,64,512]{3,2,1,0:T(8,128)(2,1)} async-done(((bf16[4,2,64,512]{3,2,1,0:T(8,128)(2,1)}), bf16[1,2,64,512]{3,2,1,0:T(8,128)(2,1)}) %reduce-scatter.19.cloned.1.call-update) | async-done | bytes 131088 | tf_op jit(solution)/shard_map/reduce_scatter | solution.py:141
  (458 shorter events, 322.9 us)
Async XLA Ops:
  7.2 33.7 %copy-start.63 = (s32[49,49]{1,0:T(8,128)S(1)}, s32[49,49]{1,0:T(8,128)}, u32[]{:S(2)}) copy-start(s32[49,49]{1,0:T(8,128)} %param.25) | copy-start | bytes 28816
  7.2 82.0 %all-gather.11.cloned.1.call-start = ((), (), s32[]{:S(2)}) async-start(), calls=%async_computation.9 | async-start | bytes 1081344 | tf_op jit(solution)/shard_map/all_gather | solution.py:100
  7.9 120.7 %all-gather.9.cloned.1.call-start = ((), (), s32[]{:S(2)}) async-start(), calls=%async_computation.8 | async-start | bytes 3244032 | tf_op jit(solution)/shard_map/all_gather | solution.py:100
  8.7 183.3 %all-gather.13.cloned.1.call-start = ((), (), s32[]{:S(2)}) async-start(), calls=%async_computation.10 | async-start | bytes 4325376 | tf_op jit(solution)/shard_map/all_gather | solution.py:100
  9.4 32.6 %copy-start.4 = (f32[392,512]{1,0:T(8,128)S(1)}, f32[392,512]{1,0:T(8,128)}, u32[]{:S(2)}) copy-start(f32[392,512]{1,0:T(8,128)} %param.15) | copy-start | bytes 2408452
  9.4 245.9 %all-gather.15.cloned.1.call-start = ((), (), s32[]{:S(2)}) async-start(), calls=%async_computation.11 | async-start | bytes 4325376 | tf_op jit(solution)/shard_map/all_gather | solution.py:100
  10.0 543.0 %all-reduce.13.cloned.1.call-start = ((), (), s32[]{:S(2)}) async-start(), calls=%async_computation.13 | async-start | bytes 8388608
  39.1 13.6 %copy-start.98 = (bf16[2,512]{1,0:T(2,128)(2,1)S(1)}, bf16[2,512]{1,0:T(2,128)(2,1)}, u32[]{:S(2)}) copy-start(bf16[2,512]{1,0:T(2,128)(2,1)} %param.22) | copy-start | bytes 6148
  88.6 175.6 %copy-start.67 = (f32[512]{0:T(512)}, f32[512]{0:T(512)S(1)}, u32[]{:S(2)}) copy-start(f32[512]{0:T(512)S(1)} %get-tuple-element.172) | copy-start | bytes 6148
  172.7 25.0 %copy-start.35 = (bf16[392,512]{0,1:T(8,128)(2,1)}, bf16[392,512]{0,1:T(8,128)(2,1)S(1)}, u32[]{:S(2)}) copy-start(bf16[392,512]{0,1:T(8,128)(2,1)S(1)} %reshape_reshape.7) | copy-start | bytes 1204228
  174.7 93.6 %copy-start.27 = (f32[392,512]{1,0:T(8,128)}, f32[392,512]{1,0:T(8,128)S(1)}, u32[]{:S(2)}) copy-start(f32[392,512]{1,0:T(8,128)S(1)} %get-tuple-element.139) | copy-start | bytes 2408452
  174.9 89.3 %copy-start.72 = (f32[392]{0:T(512)}, f32[392]{0:T(512)S(1)}, u32[]{:S(2)}) copy-start(f32[392]{0:T(512)S(1)} %add_rsqrt_fusion.2) | copy-start | bytes 4708
  312.5 9.2 %copy-start.85 = (pred[196]{0:T(512)(128)(4,1)S(1)}, pred[196]{0:T(512)(128)(4,1)}, u32[]{:S(2)}) copy-start(pred[196]{0:T(512)(128)(4,1)} %get-tuple-element.177) | copy-start | bytes 592
  333.1 9.4 %copy-start.84 = (pred[196]{0:T(512)(128)(4,1)S(1)}, pred[196]{0:T(512)(128)(4,1)}, u32[]{:S(2)}) copy-start(pred[196]{0:T(512)(128)(4,1)} %get-tuple-element.178) | copy-start | bytes 592
  391.8 9.0 %copy-start.86 = (pred[196]{0:T(512)(128)(4,1)S(1)}, pred[196]{0:T(512)(128)(4,1)}, u32[]{:S(2)}) copy-start(pred[196]{0:T(512)(128)(4,1)} %get-tuple-element.177) | copy-start | bytes 592
  473.3 134.2 %reduce-scatter.21.cloned.1.call-start = ((), (), s32[]{:S(2)}) async-start(), calls=%async_computation.6 | async-start | bytes 4718592 | tf_op jit(solution)/shard_map/reduce_scatter | solution.py:140
  502.2 159.8 %reduce-scatter.17.cloned.1.call-start = ((), (), s32[]{:S(2)}) async-start(), calls=%async_computation.4 | async-start | bytes 4718592 | tf_op jit(solution)/shard_map/reduce_scatter | solution.py:140
  522.8 269.5 %all-reduce.11.cloned.1.call-start = ((), (), s32[]{:S(2)}) async-start(), calls=%async_computation.12 | async-start | bytes 180224 | tf_op jit(solution)/shard_map/psum | solution.py:381
  525.3 82.3 %copy-start.99 = (u32[32]{0:T(128)S(1)}, u32[32]{0:T(128)}, u32[]{:S(2)}) copy-start(u32[32]{0:T(128)} %constant.99) | copy-start | bytes 388
  526.2 135.9 %copy-start.44 = (bf16[64,8,4,512]{3,1,2,0:T(8,128)(2,1)S(1)}, bf16[64,8,4,512]{3,1,2,0:T(8,128)(2,1)}, u32[]{:S(2)}) copy-start(bf16[64,8,4,512]{3,1,2,0:T(8,128)(2,1)} %copy.503) | copy-start | bytes 6291460
  526.2 135.9 %copy-start.88 = (f32[512]{0:T(512)S(1)}, f32[512]{0:T(512)}, u32[]{:S(2)}) copy-start(f32[512]{0:T(512)} %get-tuple-element.77) | copy-start | bytes 6148
  529.9 305.8 %all-reduce.15.cloned.1.call-start = ((), (), s32[]{:S(2)}) async-start(), calls=%async_computation.14 | async-start | bytes 1048576
  557.7 301.9 %reduce-scatter.23.cloned.1.call-start = ((), (), s32[]{:S(2)}) async-start(), calls=%async_computation.7 | async-start | bytes 655360 | tf_op jit(solution)/shard_map/reduce_scatter | solution.py:141
  607.5 274.4 %reduce-scatter.19.cloned.1.call-start = ((), (), s32[]{:S(2)}) async-start(), calls=%async_computation.5 | async-start | bytes 655360 | tf_op jit(solution)/shard_map/reduce_scatter | solution.py:141
  (95 other events, 235.6 us)
Sparse Core Ops, SparseCore 0:
  11.0 56.5 all-gather.10
  70.4 58.1 all-gather.8
  131.6 60.3 all-gather.12
  194.9 60.4 all-gather.14
  473.4 79.5 all-reduce.12
  556.2 51.2 reduce-scatter.20
  610.9 51.1 reduce-scatter.16
  669.3 123.0 all-reduce.10
  795.3 40.3 all-reduce.14
  837.9 21.6 reduce-scatter.22
  861.9 20.0 reduce-scatter.18
